TPU v7x, 256 devices: a whole 4x4x8 slice. The times are simulated.
256 devices in a mesh: det: 64 (over x, z, core), head: 4 (over y).
Axes of the slice: x: 4, y: 4, z: 8, core: 2. Of those that a mesh axis runs over, the one named last changes fastest.
Arguments:
- elements: bfloat16 [32768, 1024], P('det'), may hold values from -6 to 6
- element_types: int32 [32768], P('det'), may hold values from 0 to 1, as said below
- handover_counts: int32 [64, 64], replicated, may hold values from 0 to 16, as said below
- block_lists: int32 [256, 16], P('det'), may hold values from 0 to 255, as said below
- w_first: bfloat16 [2, 1024, 2048], P(None, None, 'head'), may hold values from -0.1875 to 0.1875
- w_second: bfloat16 [2, 2048, 1024], P(None, 'head'), may hold values from -0.125 to 0.125
- w_query: bfloat16 [1024, 1024], P(None, 'head'), may hold values from -3 to 3
- key_value_weight: bfloat16 [1024, 2, 256], P(None, None, 'head'), may hold values from -0.1875 to 0.1875
- attention_cotangent: bfloat16 [32768, 1024], P('det', 'head'), may hold values from -6 to 6
Outputs:
- attended: bfloat16 [32768, 1024], P('det', 'head')
- x_grad: bfloat16 [32768, 1024], P('det', 'head')
Inputs may be any that keep to these rules, and one draw needn't show every extreme that they name: `element_types`: of the 512 elements of each device of det, exactly 256 are of each type. `handover_counts`: row d, column e counts the elements that device d of det hands to device e; every row and every column sums to 512; some entries equal 16. `block_lists`: key block k is held by device k // 4 of det; the 16 entries of a query block may repeat; the lists of the 4 query blocks of one device together name exactly 1 block, counted with repeats, held by each device of det.
All inputs are finite; a program needn't handle non-finite values.
Results may differ from a plain program's by a relative error of at most 0.024.
The roundings to bfloat16 on the way count: a program that leaves them out, or rounds other values in their place, can miss the bound.
Values may be sent and summed in bfloat16 or wider, within the bound.
A program may use at most 64 MiB of HBM per device.

v0:
```python
import jax
import jax.numpy as jnp
from jax import lax
from jax.sharding import PartitionSpec as P

HEAD_SIZE = 64
BLOCK_ROWS = 128
LISTED_COUNT = 16
GROUP_HEADS = 4


def exclusive(counts, reduce_axis):
    return jnp.cumsum(counts, axis=reduce_axis, dtype=jnp.int32) - counts


def pack_rows(source_rows, starts, amounts, capacity):
    slot_ids = jnp.arange(capacity, dtype=jnp.int32)
    row_index = jnp.clip(starts[:, None] + slot_ids[None, :], 0, source_rows.shape[0] - 1)
    usable = slot_ids[None, :] < amounts[:, None]
    picked = source_rows[row_index.reshape(-1)].reshape(
        amounts.shape[0], capacity, source_rows.shape[1]
    )
    return jnp.where(usable[:, :, None], picked, jnp.zeros_like(picked))


def unpack_rows(received, starts, amounts, total_rows):
    peer_count, capacity = (received.shape[0], received.shape[1])
    within = jnp.arange(total_rows, dtype=jnp.int32)
    end_rows = starts + amounts
    peer_ids = jnp.sum(
        (end_rows[None, :] <= within[:, None]).astype(jnp.int32), axis=1, dtype=jnp.int32
    )
    slot_ids = within - starts[peer_ids]
    flattened = received.reshape(peer_count * capacity, received.shape[2])
    return flattened[peer_ids * capacity + slot_ids]


def attend(query_block_one, cotangent_block, key_block_rows, value_block_rows):
    score_scaling = HEAD_SIZE ** (-0.5)
    score_matrix = (
        jnp.einsum(
            "oenl,iel->enoi", query_block_one, key_block_rows, preferred_element_type=jnp.float32
        )
        * score_scaling
    )
    row_max = jnp.max(score_matrix, axis=-1, keepdims=True)
    exp_scores = jnp.exp(score_matrix - row_max)
    probability = exp_scores / jnp.sum(exp_scores, axis=-1, keepdims=True)
    probability_bfloat = probability.astype(jnp.bfloat16)
    attended = jnp.einsum(
        "vnys,svx->yvnx", probability_bfloat, value_block_rows, preferred_element_type=jnp.float32
    ).astype(jnp.bfloat16)
    probability_gradient = jnp.einsum(
        "oenl,iel->enoi", cotangent_block, value_block_rows, preferred_element_type=jnp.float32
    )
    row_delta = jnp.sum(probability * probability_gradient, axis=-1, keepdims=True)
    score_gradient = (probability * (probability_gradient - row_delta)).astype(jnp.bfloat16)
    query_gradient = (
        jnp.einsum(
            "vnys,svx->yvnx", score_gradient, key_block_rows, preferred_element_type=jnp.float32
        )
        * score_scaling
    ).astype(jnp.bfloat16)
    key_gradient = (
        jnp.einsum(
            "njtw,tnjs->wns", score_gradient, query_block_one, preferred_element_type=jnp.float32
        )
        * score_scaling
    )
    value_gradient = jnp.einsum(
        "njtw,tnjs->wns", probability_bfloat, cotangent_block, preferred_element_type=jnp.float32
    )
    return (attended, query_gradient, key_gradient, value_gradient)


def shards(
    elements,
    element_types,
    handover_counts,
    block_lists,
    w_first,
    w_second,
    w_query,
    key_value_weight,
    attention_cotangent,
):
    peer_count = lax.axis_size("det")
    my_index = lax.axis_index("det")
    row_count = elements.shape[0]
    model_width = elements.shape[1]
    capacity = 2 * row_count // peer_count
    starts = exclusive(handover_counts, 1)
    offsets = exclusive(handover_counts, 0)
    send_starts = lax.dynamic_index_in_dim(starts, my_index, 0, keepdims=False)
    send_counts = lax.dynamic_index_in_dim(handover_counts, my_index, 0, keepdims=False)
    recv_starts = lax.dynamic_index_in_dim(offsets, my_index, 1, keepdims=False)
    recv_counts = lax.dynamic_index_in_dim(handover_counts, my_index, 1, keepdims=False)
    type_count = w_first.shape[0]
    per_type = row_count // type_count
    type_order = jnp.argsort(element_types, stable=True)
    back_order = (
        jnp.zeros_like(type_order).at[type_order].set(jnp.arange(row_count, dtype=jnp.int32))
    )
    sorted_rows = elements[type_order].reshape(type_count, per_type, model_width)
    preact = jnp.einsum("trd,tdh->trh", sorted_rows, w_first, preferred_element_type=jnp.float32)
    hidden = jax.nn.gelu(preact).astype(jnp.bfloat16)
    sorted_mlp = jnp.einsum("trh,thd->trd", hidden, w_second, preferred_element_type=jnp.float32)
    partial_mlp = sorted_mlp.reshape(row_count, model_width)[back_order]
    mlp_sum = lax.psum(partial_mlp, "head")
    mixed = (elements.astype(jnp.float32) + mlp_sum).astype(jnp.bfloat16)
    outbound = pack_rows(mixed, send_starts, send_counts, capacity)
    inbound = lax.all_to_all(outbound, "det", split_axis=0, concat_axis=0, tiled=True)
    moved = unpack_rows(inbound, recv_starts, recv_counts, row_count)
    kv_width = key_value_weight.shape[2]
    key_value_flat = key_value_weight.reshape(model_width, 2 * kv_width)
    query_rows_all = jnp.dot(moved, w_query, preferred_element_type=jnp.float32).astype(
        jnp.bfloat16
    )
    key_value_pairs = jnp.dot(moved, key_value_flat, preferred_element_type=jnp.float32).astype(
        jnp.bfloat16
    )
    blocks_dev = row_count // BLOCK_ROWS
    slot_count = blocks_dev * LISTED_COUNT
    per_pair = slot_count // peer_count
    flat_list = block_lists.reshape(slot_count)
    owners = flat_list // blocks_dev
    local_ids = flat_list % blocks_dev
    slot_order = jnp.arange(slot_count, dtype=jnp.int32)
    earlier = (owners[:, None] == owners[None, :]) & (slot_order[None, :] < slot_order[:, None])
    slot_rank = jnp.sum(earlier.astype(jnp.int32), axis=1, dtype=jnp.int32)
    position = owners * per_pair + slot_rank
    requests = (
        jnp.zeros((slot_count,), jnp.int32)
        .at[position]
        .set(local_ids)
        .reshape(peer_count, per_pair)
    )
    wanted = lax.all_to_all(requests, "det", split_axis=0, concat_axis=0, tiled=True)
    all_keys = lax.all_gather(key_value_pairs, "det", axis=0, tiled=True)
    listed = all_keys.reshape(-1, BLOCK_ROWS, 2 * kv_width)[flat_list]
    listed = listed.reshape(blocks_dev, LISTED_COUNT * BLOCK_ROWS, 2 * kv_width)
    kv_heads = kv_width // HEAD_SIZE
    query_block_list = query_rows_all.reshape(
        blocks_dev, BLOCK_ROWS, kv_heads, GROUP_HEADS, HEAD_SIZE
    )
    cotangent_blocks = attention_cotangent.reshape(
        blocks_dev, BLOCK_ROWS, kv_heads, GROUP_HEADS, HEAD_SIZE
    )

    def one_block(inputs):
        query_block_one, cotangent_block, key_value_rows = inputs
        key_block_rows = key_value_rows[:, :kv_width].reshape(
            LISTED_COUNT * BLOCK_ROWS, kv_heads, HEAD_SIZE
        )
        value_block_rows = key_value_rows[:, kv_width:].reshape(
            LISTED_COUNT * BLOCK_ROWS, kv_heads, HEAD_SIZE
        )
        return attend(query_block_one, cotangent_block, key_block_rows, value_block_rows)

    attended, query_gradient, key_gradient, value_gradient = lax.map(
        one_block, (query_block_list, cotangent_blocks, listed)
    )
    slot_gradients = jnp.concatenate(
        [
            key_gradient.reshape(blocks_dev, LISTED_COUNT * BLOCK_ROWS, kv_width),
            value_gradient.reshape(blocks_dev, LISTED_COUNT * BLOCK_ROWS, kv_width),
        ],
        axis=2,
    )
    slot_gradients = slot_gradients.reshape(slot_count, BLOCK_ROWS, 2 * kv_width).astype(
        jnp.bfloat16
    )
    returned = (
        jnp.zeros_like(slot_gradients)
        .at[position]
        .set(slot_gradients)
        .reshape(peer_count, per_pair, BLOCK_ROWS, 2 * kv_width)
    )
    collected = lax.all_to_all(returned, "det", split_axis=0, concat_axis=0, tiled=True)
    collected = collected.reshape(slot_count, BLOCK_ROWS, 2 * kv_width).astype(jnp.float32)
    key_gradient_total = (
        jnp.zeros((blocks_dev, BLOCK_ROWS, 2 * kv_width), jnp.float32)
        .at[wanted.reshape(-1)]
        .add(collected)
    )
    key_bfloat = key_gradient_total.reshape(row_count, 2 * kv_width).astype(jnp.bfloat16)
    contract = (((1,), (1,)), ((), ()))
    partial_back = lax.dot_general(
        query_gradient.reshape(row_count, -1), w_query, contract, preferred_element_type=jnp.float32
    )
    partial_back = partial_back + lax.dot_general(
        key_bfloat, key_value_flat, contract, preferred_element_type=jnp.float32
    )
    back_sum = lax.psum(partial_back, "head").astype(jnp.bfloat16)
    outbound_back = pack_rows(back_sum, recv_starts, recv_counts, capacity)
    inbound_back = lax.all_to_all(outbound_back, "det", split_axis=0, concat_axis=0, tiled=True)
    upstream = unpack_rows(inbound_back, send_starts, send_counts, row_count)
    sorted_up = upstream[type_order].reshape(type_count, per_type, model_width)
    hidden_grad = jnp.einsum(
        "trd,thd->trh", sorted_up, w_second, preferred_element_type=jnp.float32
    )
    preact_grad = jax.vjp(jax.nn.gelu, preact)[1](hidden_grad)[0].astype(jnp.bfloat16)
    sorted_input = jnp.einsum(
        "trh,tdh->trd", preact_grad, w_first, preferred_element_type=jnp.float32
    )
    input_part = sorted_input.reshape(row_count, model_width)[back_order]
    input_share = lax.psum_scatter(input_part, "head", scatter_dimension=1, tiled=True)
    share_width = input_share.shape[1]
    own_upstream = lax.dynamic_slice_in_dim(
        upstream, lax.axis_index("head") * share_width, share_width, 1
    )
    x_grad = (own_upstream.astype(jnp.float32) + input_share).astype(jnp.bfloat16)
    return (attended.reshape(row_count, -1), x_grad)


def solution(mesh):
    return jax.shard_map(
        shards,
        mesh=mesh,
        in_specs=(
            P("det", None),
            P("det"),
            P(),
            P("det", None),
            P(None, None, "head"),
            P(None, "head", None),
            P(None, "head"),
            P(None, None, "head"),
            P("det", "head"),
        ),
        out_specs=(P("det", "head"), P("det", "head")),
        check_vma=False,
    )
```

profile of v0, /device:TPU:1, one launch (start us, length us, event | category | flops | bytes accessed | tf_op | source)
XLA Modules:
  0.0 602.9 jit_solution(14626544373594868727)
XLA Ops:
  22.9 5.3 gather_fusion.1
  29.4 66.3 %all-reduce.3.cloned.1.call-done = f32[512,1024]{1,0:T(8,128)} async-done(((f32[512,1024]{1,0:T(8,128)}), f32[512,1024]{1,0:T(8,128)}) %all-reduce.3.cloned.1.call-update) | async-done | bytes 2097168 | tf_op jit(solution)/shard_map/psum | solution.py:109
  98.0 5.4 gather_fusion.2
  106.6 11.0 %all-to-all-start = ((bf16[64,16,1024]{2,1,0:T(8,128)(2,1)}), bf16[64,16,1024]{2,1,0:T(8,128)(2,1)}, u32[]{:S(2)}, u32[]{:S(2)}) async-start(bf16[64,16,1024]{2,1,0:T(8,128)(2,1)} %broadcast_select_fusion.1), calls=%async_computation | async-start | bytes 4194304 | tf_op jit(solution)/shard_map/all_to_all | solution.py:112
  132.9 35.3 %select_select_fusion.1 = s32[512]{0:T(512)S(1)} fusion(pred[512]{0:T(512)(128)(4,1)S(1)} %get-tuple-element.224, pred[512]{0:T(512)(128)(4,1)S(1)} %get-tuple-element.223, pred[512]{0:T(512)(128)(4,1)S(1)} %get-tuple-element.222, pred[512]{0:T(512)(128)(4,1)S(1)} %get-tuple-element.221, pred[512]{0:T(512)(128)(4,1)S(1)} %get-tuple-element.220, ...), kind=kLoop, calls=%fused_computation.250 | loop fusion | flops 29184 | bytes 33508 | tf_op jit(solution)/shard_map/gather | solution.py:33
  168.3 35.6 %select_select_fusion = s32[512]{0:T(512)S(1)} fusion(pred[512]{0:T(512)(128)(4,1)S(1)} %get-tuple-element.167, pred[512]{0:T(512)(128)(4,1)S(1)} %get-tuple-element.166, pred[512]{0:T(512)(128)(4,1)S(1)} %get-tuple-element.165, pred[512]{0:T(512)(128)(4,1)S(1)} %get-tuple-element.164, pred[512]{0:T(512)(128)(4,1)S(1)} %get-tuple-element.163, ...), kind=kLoop, calls=%fused_computation.249 | loop fusion | flops 29184 | bytes 33508 | tf_op jit(solution)/shard_map/gather | solution.py:33
  204.0 4.6 gather_fusion.3
  210.1 10.0 %scatter_custom_fusion.1 = s32[64]{0:T(128)S(1)} fusion(s32[64]{0:T(128)S(1)} %get-tuple-element.385, s32[64]{0:T(128)S(1)} %get-tuple-element.383, s32[]{:T(128)} %constant.56.clone.1), kind=kCustom, calls=%fused_computation.271 | custom fusion | bytes 260 | tf_op jit(solution)/shard_map/scatter | solution.py:135
  220.8 10.3 %all-to-all-start.1 = ((s32[64,1,1]{2,1,0:T(1,128)}), s32[64,1,1]{2,1,0:T(1,128)S(1)}, u32[]{:S(2)}, u32[]{:S(2)}) async-start(s32[64,1,1]{2,1,0:T(1,128)} %copy.91), calls=%async_computation.1 | async-start | bytes 65536 | tf_op jit(solution)/shard_map/all_to_all | solution.py:138
  237.2 55.5 %all-gather.2.cloned.1.call-done = bf16[32768,128]{1,0:T(8,128)(2,1)} async-done(((bf16[512,128]{1,0:T(8,128)(2,1)}), bf16[32768,128]{1,0:T(8,128)(2,1)}) %all-gather.2.cloned.1.call-update) | async-done | bytes 8388624 | tf_op jit(solution)/shard_map/all_gather | solution.py:139
  292.7 5.6 gather_fusion.4
  298.3 41.0 %while.16 = (s32[]{:T(128)}, bf16[4,128,1,4,64]{1,4,3,2,0:T(8,128)(2,1)}, bf16[4,128,1,4,64]{1,4,3,2,0:T(8,128)(2,1)}, bf16[4,2048,1,64]{1,3,2,0:T(8,128)(2,1)},...) while((s32[]{:T(128)}, ...), condition=%wide.region_10.11_spmd, body=%wide.region_6.10_spmd.sunk | while | flops 830700032 | bytes 62289140 | solution.py:160
  355.6 10.0 %scatter_fusion = bf16[64,128,128]{2,1,0:T(8,128)(2,1)} fusion(bf16[64,128,128]{2,1,0:T(8,128)(2,1)} %broadcast_in_dim.43, s32[64]{0:T(128)S(1)} %get-tuple-element.385, bf16[64,128,128]{2,1,0:T(8,128)(2,1)} %copy.94), kind=kCustom, calls=%fused_computation.11 | custom fusion | bytes 6291712 | tf_op jit(solution)/shard_map/scatter | solution.py:176
  365.6 6.0 %all-to-all-start.2 = ((bf16[64,1,128,128]{3,2,1,0:T(8,128)(2,1)}), bf16[64,1,128,128]{3,2,1,0:T(8,128)(2,1)}, u32[]{:S(2)}, u32[]{:S(2)}) async-start(bf16[64,1,128,128]{3,2,1,0:T(8,128)(2,1)} %bitcast.379), calls=%async_computation.2 | async-start | bytes 4194304 | tf_op jit(solution)/shard_map/all_to_all | solution.py:179
  373.3 49.4 %all-to-all-done.2 = bf16[64,1,128,128]{3,2,1,0:T(8,128)(2,1)} async-done(((bf16[64,1,128,128]{3,2,1,0:T(8,128)(2,1)}), bf16[64,1,128,128]{3,2,1,0:T(8,128)(2,1)}, u32[]{:S(2)}, u32[]{:S(2)}) %all-to-all-start.2) | async-done | bytes 2097184 | tf_op jit(solution)/shard_map/all_to_all | solution.py:179
  426.8 8.8 %scatter_fusion.1 = f32[4,128,128]{2,1,0:T(8,128)S(1)} fusion(f32[4,128,128]{2,1,0:T(8,128)S(1)} %broadcast_in_dim.42, s32[64]{0:T(128)S(1)} %fusion.73, f32[64,128,128]{2,1,0:T(8,128)} %bitcast_convert_fusion), kind=kCustom, calls=%fused_computation.12 | custom fusion | flops 1048576 | bytes 12583168 | tf_op jit(solution)/shard_map/scatter-add | solution.py:184
  438.5 42.7 %all-reduce.4 = bf16[512,1024]{1,0:T(8,128)(2,1)S(1)} all-reduce(f32[512,1024]{1,0:T(8,128)} %convolution_add_fusion), channel_id=1, replica_groups=mesh['det'=64,'head'=4] {'head'}, use_global_device_ids=true, to_apply=%region_15.16 | all-reduce | flops 524288 | bytes 3145728 | tf_op jit(solution)/shard_map/psum | solution.py:194
  481.2 5.4 gather_fusion.5
  489.8 8.1 %all-to-all-start.3 = ((bf16[64,16,1024]{2,1,0:T(8,128)(2,1)}), bf16[64,16,1024]{2,1,0:T(8,128)(2,1)}, u32[]{:S(2)}, u32[]{:S(2)}) async-start(bf16[64,16,1024]{2,1,0:T(8,128)(2,1)} %broadcast_select_fusion), calls=%async_computation.3 | async-start | bytes 4194304 | tf_op jit(solution)/shard_map/all_to_all | solution.py:196
  497.9 51.1 %all-to-all-done.3 = bf16[64,16,1024]{2,1,0:T(8,128)(2,1)} async-done(((bf16[64,16,1024]{2,1,0:T(8,128)(2,1)}), bf16[64,16,1024]{2,1,0:T(8,128)(2,1)}, u32[]{:S(2)}, u32[]{:S(2)}) %all-to-all-start.3) | async-done | bytes 2097184 | tf_op jit(solution)/shard_map/all_to_all | solution.py:196
  548.9 4.6 gather_fusion.6
  556.3 5.3 fusion.53
  561.7 5.2 gather_fusion.8
  571.1 23.1 %reduce-scatter.2.cloned.1.call-done = f32[512,256]{1,0:T(8,128)} async-done(((f32[512,1024]{1,0:T(8,128)}), f32[512,256]{1,0:T(8,128)}) %reduce-scatter.2.cloned.1.call-update) | async-done | bytes 524304 | tf_op jit(solution)/shard_map/reduce_scatter | solution.py:207
  (196 shorter events, 123.4 us)
Async XLA Ops:
  7.2 13.6 %copy-start = (bf16[2,512,1024]{2,1,0:T(8,128)(2,1)S(1)}, bf16[2,512,1024]{2,1,0:T(8,128)(2,1)}, u32[]{:S(2)}) copy-start(bf16[2,512,1024]{2,1,0:T(8,128)(2,1)} %param.16) | copy-start | bytes 6291460
  7.2 88.6 %all-reduce.3.cloned.1.call-start = ((), (), s32[]{:S(2)}) async-start(), calls=%async_computation.5 | async-start | bytes 4194304 | tf_op jit(solution)/shard_map/psum | solution.py:109
  11.8 6.6 %copy-start.13 = (s32[1024]{0:T(1024)}, s32[1024]{0:T(1024)S(1)}, u32[]{:S(2)}) copy-start(s32[1024]{0:T(1024)S(1)} %pad_clamp_fusion.4) | copy-start | bytes 12292
  14.3 8.6 %copy-start.15 = (s32[1024]{0:T(1024)}, s32[1024]{0:T(1024)S(1)}, u32[]{:S(2)}) copy-start(s32[1024]{0:T(1024)S(1)} %pad_clamp_fusion.3) | copy-start | bytes 12292
  20.7 2.2 copy-start.1
  106.6 97.4 %all-to-all-start = ((bf16[64,16,1024]{2,1,0:T(8,128)(2,1)}), bf16[64,16,1024]{2,1,0:T(8,128)(2,1)}, u32[]{:S(2)}, u32[]{:S(2)}) async-start(bf16[64,16,1024]{2,1,0:T(8,128)(2,1)} %broadcast_select_fusion.1), calls=%async_computation | async-start | bytes 4194304 | tf_op jit(solution)/shard_map/all_to_all | solution.py:112
  117.6 175.2 %all-gather.2.cloned.1.call-start = ((), (), s32[]{:S(2)}) async-start(), calls=%async_computation.6 | async-start | bytes 8519680 | tf_op jit(solution)/shard_map/all_gather | solution.py:139
  203.9 4.7 copy-start.6
  204.0 5.8 copy-start.17
  220.8 144.7 %all-to-all-start.1 = ((s32[64,1,1]{2,1,0:T(1,128)}), s32[64,1,1]{2,1,0:T(1,128)S(1)}, u32[]{:S(2)}, u32[]{:S(2)}) async-start(s32[64,1,1]{2,1,0:T(1,128)} %copy.91), calls=%async_computation.1 | async-start | bytes 65536 | tf_op jit(solution)/shard_map/all_to_all | solution.py:138
  302.6 1.3 copy-start.5
  310.7 1.3 copy-start.10
  312.9 1.3 copy-start.5
  320.9 1.3 copy-start.10
  323.1 1.3 copy-start.5
  331.2 1.3 copy-start.10
  333.4 1.3 copy-start.5
  365.6 7.6 %copy-start.12 = (bf16[4,128,1,4,64]{1,4,3,2,0:T(8,128)(2,1)S(1)}, bf16[4,128,1,4,64]{1,4,3,2,0:T(8,128)(2,1)}, u32[]{:S(2)}) copy-start(bf16[4,128,1,4,64]{1,4,3,2,0:T(8,128)(2,1)} %get-tuple-element.50) | copy-start | bytes 786436
  365.6 57.2 %all-to-all-start.2 = ((bf16[64,1,128,128]{3,2,1,0:T(8,128)(2,1)}), bf16[64,1,128,128]{3,2,1,0:T(8,128)(2,1)}, u32[]{:S(2)}, u32[]{:S(2)}) async-start(bf16[64,1,128,128]{3,2,1,0:T(8,128)(2,1)} %bitcast.379), calls=%async_computation.2 | async-start | bytes 4194304 | tf_op jit(solution)/shard_map/all_to_all | solution.py:179
  426.8 8.8 %copy-start.7 = (bf16[1024,2,64]{0,2,1:T(8,128)(2,1)S(1)}, bf16[1024,2,64]{0,2,1:T(8,128)(2,1)}, u32[]{:S(2)}) copy-start(bf16[1024,2,64]{0,2,1:T(8,128)(2,1)} %param.18) | copy-start | bytes 786436
  489.8 59.2 %all-to-all-start.3 = ((bf16[64,16,1024]{2,1,0:T(8,128)(2,1)}), bf16[64,16,1024]{2,1,0:T(8,128)(2,1)}, u32[]{:S(2)}, u32[]{:S(2)}) async-start(bf16[64,16,1024]{2,1,0:T(8,128)(2,1)} %broadcast_select_fusion), calls=%async_computation.3 | async-start | bytes 4194304 | tf_op jit(solution)/shard_map/all_to_all | solution.py:196
  497.8 96.4 %reduce-scatter.2.cloned.1.call-start = ((), (), s32[]{:S(2)}) async-start(), calls=%async_computation.7 | async-start | bytes 2621440 | tf_op jit(solution)/shard_map/reduce_scatter | solution.py:207
  548.9 4.6 copy-start.14
  556.3 5.3 copy-start.16
  (16 other events, 18.3 us)
Sparse Core Ops, SparseCore 0:
  28.3 67.4 all-reduce.2
  209.9 82.8 all-gather.1
  567.0 27.1 reduce-scatter.1
where the time goes:
time: 614 us; the launch traced here: 603 us
  waiting for transfers between devices  245 us (40%)
  other arithmetic  121 us (20%)
  local copies, waits for them, and re-layouts  103 us (17%)
  blocking collectives  42.7 us (7%)
  matrix products  40.3 us (7%)
  starting transfers between devices  35.6 us (6%)
  between operations  14.6 us (2%)
    gather x6, other arithmetic, unpack_rows(): slot_ids = within - starts[peer_ids]  80.3 us
    psum x1, waiting for transfers between devices, shards(): mlp_sum = lax.psum(partial_mlp, 'head')  66.3 us
    all_gather x1, waiting for transfers between devices, shards(): all_keys = lax.all_gather(key_value_pairs, 'det', axis=0, tiled=True)  55.5 us
    all_to_all x1, waiting for transfers between devices, shards(): lax.all_to_all(outbound_back, 'det', split_axis=0, concat_axis=0, tiled=T...  51.1 us
    all_to_all x1, waiting for transfers between devices, shards(): lax.all_to_all(returned, 'det', split_axis=0, concat_axis=0, tiled=True)  49.4 us
    psum x1, blocking collectives, shards(): back_sum = lax.psum(partial_back, 'head').astype(jnp.bfloat16)  42.7 us
    reduce_scatter x1, waiting for transfers between devices, shards(): lax.psum_scatter(input_part, 'head', scatter_dimension=1, tiled=True)  23.1 us
  transfers between devices with their start and end apart: 7, of which 5 were waited for; matrix products, arithmetic and copies ran while one was open for 30% of the time, Pallas kernels for 0%

commit v1 on v0

--- a/solution.py
+++ b/solution.py
@@ -106,7 +106,7 @@
     hidden = jax.nn.gelu(preact).astype(jnp.bfloat16)
     sorted_mlp = jnp.einsum("trh,thd->trd", hidden, w_second, preferred_element_type=jnp.float32)
     partial_mlp = sorted_mlp.reshape(row_count, model_width)[back_order]
-    mlp_sum = lax.psum(partial_mlp, "head")
+    mlp_sum = jnp.sum(lax.all_gather(partial_mlp, "head"), axis=0)
     mixed = (elements.astype(jnp.float32) + mlp_sum).astype(jnp.bfloat16)
     outbound = pack_rows(mixed, send_starts, send_counts, capacity)
     inbound = lax.all_to_all(outbound, "det", split_axis=0, concat_axis=0, tiled=True)

time: 614 us -> 642 us (1.046)
  waiting for transfers between devices: 245 us -> 277 us
  local copies, waits for them, and re-layouts: 103 us -> 93.8 us
    all_gather x0 -> x1, waiting for transfers between devices: none -> 88.2 us  [shards(): mlp_sum = jnp.sum(lax.all_gather(partial_mlp, 'head'), axis=0)]
    psum x1 -> x0, waiting for transfers between devices: 66.3 us -> none  [shards(): mlp_sum = lax.psum(partial_mlp, 'head')]
    all_gather x1, waiting for transfers between devices: 55.5 us -> 65.6 us  [shards(): all_keys = lax.all_gather(key_value_pairs, 'det', axis=0, tiled=True)]
    scatter x1, local copies, waits for them, and re-layouts: 10 us -> 0.77 us  [shards(): requests = jnp.zeros((slot_count,), jnp.int32).at[position].set(local_ids...]
  transfers between devices with their start and end apart: 7 -> 7, of which waited for: 5 -> 5; matrix products, arithmetic and copies ran while one was open for 30% -> 27% of each run, Pallas kernels for 0% -> 0%
where the time goes in v1:
time: 642 us; the launch traced here: 632 us
  waiting for transfers between devices  277 us (43%)
  other arithmetic  127 us (20%)
  local copies, waits for them, and re-layouts  93.8 us (15%)
  blocking collectives  42.7 us (7%)
  matrix products  40.4 us (6%)
  starting transfers between devices  36.3 us (6%)
  between operations  14.5 us (2%)
    all_gather x1, waiting for transfers between devices, shards(): mlp_sum = jnp.sum(lax.all_gather(partial_mlp, 'head'), axis=0)  88.2 us
    gather x6, other arithmetic, unpack_rows(): slot_ids = within - starts[peer_ids]  80.3 us
    all_gather x1, waiting for transfers between devices, shards(): all_keys = lax.all_gather(key_value_pairs, 'det', axis=0, tiled=True)  65.6 us
    all_to_all x1, waiting for transfers between devices, shards(): lax.all_to_all(outbound_back, 'det', split_axis=0, concat_axis=0, tiled=T...  51.1 us
    all_to_all x1, waiting for transfers between devices, shards(): lax.all_to_all(returned, 'det', split_axis=0, concat_axis=0, tiled=True)  49.4 us
    psum x1, blocking collectives, shards(): back_sum = lax.psum(partial_back, 'head').astype(jnp.bfloat16)  42.7 us
    reduce_scatter x1, waiting for transfers between devices, shards(): lax.psum_scatter(input_part, 'head', scatter_dimension=1, tiled=True)  23.1 us
  transfers between devices with their start and end apart: 7, of which 5 were waited for; matrix products, arithmetic and copies ran while one was open for 27% of the time, Pallas kernels for 0%

profile of v1, /device:TPU:1, one launch (start us, length us, event | category | flops | bytes accessed | tf_op | source)
XLA Modules:
  0.0 632.2 jit_solution(91101449474358885)
XLA Ops:
  23.0 5.2 gather_fusion.1
  29.5 88.2 %all-gather.6.cloned.1.call-done = f32[2048,1024]{1,0:T(8,128)} async-done(((f32[512,1024]{1,0:T(8,128)}), f32[2048,1024]{1,0:T(8,128)}) %all-gather.6.cloned.1.call-update) | async-done | bytes 8388624 | tf_op jit(solution)/shard_map/all_gather | solution.py:109
  117.6 6.0 reduce_sum.60
  125.8 5.4 gather_fusion.2
  134.4 11.0 %all-to-all-start = ((bf16[64,16,1024]{2,1,0:T(8,128)(2,1)}), bf16[64,16,1024]{2,1,0:T(8,128)(2,1)}, u32[]{:S(2)}, u32[]{:S(2)}) async-start(bf16[64,16,1024]{2,1,0:T(8,128)(2,1)} %broadcast_select_fusion.1), calls=%async_computation | async-start | bytes 4194304 | tf_op jit(solution)/shard_map/all_to_all | solution.py:112
  161.2 35.3 %select_select_fusion.1 = s32[512]{0:T(512)S(1)} fusion(pred[512]{0:T(512)(128)(4,1)S(1)} %get-tuple-element.224, pred[512]{0:T(512)(128)(4,1)S(1)} %get-tuple-element.223, pred[512]{0:T(512)(128)(4,1)S(1)} %get-tuple-element.222, pred[512]{0:T(512)(128)(4,1)S(1)} %get-tuple-element.221, pred[512]{0:T(512)(128)(4,1)S(1)} %get-tuple-element.220, ...), kind=kLoop, calls=%fused_computation.250 | loop fusion | flops 29184 | bytes 33508 | tf_op jit(solution)/shard_map/gather | solution.py:33
  196.5 35.6 %select_select_fusion = s32[512]{0:T(512)S(1)} fusion(pred[512]{0:T(512)(128)(4,1)S(1)} %get-tuple-element.167, pred[512]{0:T(512)(128)(4,1)S(1)} %get-tuple-element.166, pred[512]{0:T(512)(128)(4,1)S(1)} %get-tuple-element.165, pred[512]{0:T(512)(128)(4,1)S(1)} %get-tuple-element.164, pred[512]{0:T(512)(128)(4,1)S(1)} %get-tuple-element.163, ...), kind=kLoop, calls=%fused_computation.249 | loop fusion | flops 29184 | bytes 33508 | tf_op jit(solution)/shard_map/gather | solution.py:33
  232.2 4.6 gather_fusion.3
  239.9 10.6 %all-to-all-start.1 = ((s32[64,1,1]{2,1,0:T(1,128)}), s32[64,1,1]{2,1,0:T(1,128)S(1)}, u32[]{:S(2)}, u32[]{:S(2)}) async-start(s32[64,1,1]{2,1,0:T(1,128)} %copy.91), calls=%async_computation.1 | async-start | bytes 65536 | tf_op jit(solution)/shard_map/all_to_all | solution.py:138
  256.5 65.6 %all-gather.4.cloned.1.call-done = bf16[32768,128]{1,0:T(8,128)(2,1)} async-done(((bf16[512,128]{1,0:T(8,128)(2,1)}), bf16[32768,128]{1,0:T(8,128)(2,1)}) %all-gather.4.cloned.1.call-update) | async-done | bytes 8388624 | tf_op jit(solution)/shard_map/all_gather | solution.py:139
  322.2 5.6 gather_fusion.4
  327.8 41.0 %while.16 = (s32[]{:T(128)}, bf16[4,128,1,4,64]{1,4,3,2,0:T(8,128)(2,1)}, bf16[4,128,1,4,64]{1,4,3,2,0:T(8,128)(2,1)}, bf16[4,2048,1,64]{1,3,2,0:T(8,128)(2,1)},...) while((s32[]{:T(128)}, ...), condition=%wide.region_10.11_spmd, body=%wide.region_6.10_spmd.sunk | while | flops 830700032 | bytes 62289140 | solution.py:160
  385.0 10.0 %scatter_fusion = bf16[64,128,128]{2,1,0:T(8,128)(2,1)} fusion(bf16[64,128,128]{2,1,0:T(8,128)(2,1)} %broadcast_in_dim.43, s32[64]{0:T(128)S(1)} %get-tuple-element.385, bf16[64,128,128]{2,1,0:T(8,128)(2,1)} %copy.94), kind=kCustom, calls=%fused_computation.11 | custom fusion | bytes 6291712 | tf_op jit(solution)/shard_map/scatter | solution.py:176
  395.0 6.1 all-to-all-start.2
  402.8 49.4 %all-to-all-done.2 = bf16[64,1,128,128]{3,2,1,0:T(8,128)(2,1)} async-done(((bf16[64,1,128,128]{3,2,1,0:T(8,128)(2,1)}), bf16[64,1,128,128]{3,2,1,0:T(8,128)(2,1)}, u32[]{:S(2)}, u32[]{:S(2)}) %all-to-all-start.2) | async-done | bytes 2097184 | tf_op jit(solution)/shard_map/all_to_all | solution.py:179
  456.3 8.8 %scatter_fusion.1 = f32[4,128,128]{2,1,0:T(8,128)S(1)} fusion(f32[4,128,128]{2,1,0:T(8,128)S(1)} %broadcast_in_dim.42, s32[64]{0:T(128)S(1)} %fusion.73, f32[64,128,128]{2,1,0:T(8,128)} %bitcast_convert_fusion), kind=kCustom, calls=%fused_computation.12 | custom fusion | flops 1048576 | bytes 12583168 | tf_op jit(solution)/shard_map/scatter-add | solution.py:184
  467.9 42.7 %all-reduce.1 = bf16[512,1024]{1,0:T(8,128)(2,1)S(1)} all-reduce(f32[512,1024]{1,0:T(8,128)} %convolution_add_fusion), channel_id=1, replica_groups=mesh['det'=64,'head'=4] {'head'}, use_global_device_ids=true, to_apply=%region_15.16 | all-reduce | flops 524288 | bytes 3145728 | tf_op jit(solution)/shard_map/psum | solution.py:194
  510.6 5.4 gather_fusion.5
  519.2 8.1 %all-to-all-start.3 = ((bf16[64,16,1024]{2,1,0:T(8,128)(2,1)}), bf16[64,16,1024]{2,1,0:T(8,128)(2,1)}, u32[]{:S(2)}, u32[]{:S(2)}) async-start(bf16[64,16,1024]{2,1,0:T(8,128)(2,1)} %broadcast_select_fusion), calls=%async_computation.3 | async-start | bytes 4194304 | tf_op jit(solution)/shard_map/all_to_all | solution.py:196
  527.3 51.1 %all-to-all-done.3 = bf16[64,16,1024]{2,1,0:T(8,128)(2,1)} async-done(((bf16[64,16,1024]{2,1,0:T(8,128)(2,1)}), bf16[64,16,1024]{2,1,0:T(8,128)(2,1)}, u32[]{:S(2)}, u32[]{:S(2)}) %all-to-all-start.3) | async-done | bytes 2097184 | tf_op jit(solution)/shard_map/all_to_all | solution.py:196
  578.4 4.6 gather_fusion.6
  585.8 5.3 fusion.53
  591.1 5.2 gather_fusion.8
  600.5 23.1 %reduce-scatter.2.cloned.1.call-done = f32[512,256]{1,0:T(8,128)} async-done(((f32[512,1024]{1,0:T(8,128)}), f32[512,256]{1,0:T(8,128)}) %reduce-scatter.2.cloned.1.call-update) | async-done | bytes 524304 | tf_op jit(solution)/shard_map/reduce_scatter | solution.py:207
  (197 shorter events, 124.7 us)
Async XLA Ops:
  7.2 13.6 %copy-start = (bf16[2,512,1024]{2,1,0:T(8,128)(2,1)S(1)}, bf16[2,512,1024]{2,1,0:T(8,128)(2,1)}, u32[]{:S(2)}) copy-start(bf16[2,512,1024]{2,1,0:T(8,128)(2,1)} %param.16) | copy-start | bytes 6291460
  7.2 110.4 %all-gather.6.cloned.1.call-start = ((), (), s32[]{:S(2)}) async-start(), calls=%async_computation.7 | async-start | bytes 10485760 | tf_op jit(solution)/shard_map/all_gather | solution.py:109
  11.8 6.6 %copy-start.13 = (s32[1024]{0:T(1024)}, s32[1024]{0:T(1024)S(1)}, u32[]{:S(2)}) copy-start(s32[1024]{0:T(1024)S(1)} %pad_clamp_fusion.4) | copy-start | bytes 12292
  14.3 8.7 %copy-start.15 = (s32[1024]{0:T(1024)}, s32[1024]{0:T(1024)S(1)}, u32[]{:S(2)}) copy-start(s32[1024]{0:T(1024)S(1)} %pad_clamp_fusion.3) | copy-start | bytes 12292
  20.7 2.3 copy-start.1
  134.4 97.8 %all-to-all-start = ((bf16[64,16,1024]{2,1,0:T(8,128)(2,1)}), bf16[64,16,1024]{2,1,0:T(8,128)(2,1)}, u32[]{:S(2)}, u32[]{:S(2)}) async-start(bf16[64,16,1024]{2,1,0:T(8,128)(2,1)} %broadcast_select_fusion.1), calls=%async_computation | async-start | bytes 4194304 | tf_op jit(solution)/shard_map/all_to_all | solution.py:112
  145.4 176.8 %all-gather.4.cloned.1.call-start = ((), (), s32[]{:S(2)}) async-start(), calls=%async_computation.5 | async-start | bytes 8519680 | tf_op jit(solution)/shard_map/all_gather | solution.py:139
  232.2 4.7 copy-start.6
  232.2 5.8 copy-start.17
  239.9 155.1 %all-to-all-start.1 = ((s32[64,1,1]{2,1,0:T(1,128)}), s32[64,1,1]{2,1,0:T(1,128)S(1)}, u32[]{:S(2)}, u32[]{:S(2)}) async-start(s32[64,1,1]{2,1,0:T(1,128)} %copy.91), calls=%async_computation.1 | async-start | bytes 65536 | tf_op jit(solution)/shard_map/all_to_all | solution.py:138
  329.8 1.3 copy-start.10
  332.1 1.3 copy-start.5
  340.1 1.3 copy-start.10
  342.3 1.3 copy-start.5
  350.3 1.3 copy-start.10
  352.6 1.3 copy-start.5
  362.8 1.3 copy-start.5
  395.0 7.6 %copy-start.12 = (bf16[4,128,1,4,64]{1,4,3,2,0:T(8,128)(2,1)S(1)}, bf16[4,128,1,4,64]{1,4,3,2,0:T(8,128)(2,1)}, u32[]{:S(2)}) copy-start(bf16[4,128,1,4,64]{1,4,3,2,0:T(8,128)(2,1)} %get-tuple-element.50) | copy-start | bytes 786436
  395.0 57.2 %all-to-all-start.2 = ((bf16[64,1,128,128]{3,2,1,0:T(8,128)(2,1)}), bf16[64,1,128,128]{3,2,1,0:T(8,128)(2,1)}, u32[]{:S(2)}, u32[]{:S(2)}) async-start(bf16[64,1,128,128]{3,2,1,0:T(8,128)(2,1)} %bitcast.380), calls=%async_computation.2 | async-start | bytes 4194304 | tf_op jit(solution)/shard_map/all_to_all | solution.py:179
  456.2 8.8 %copy-start.7 = (bf16[1024,2,64]{0,2,1:T(8,128)(2,1)S(1)}, bf16[1024,2,64]{0,2,1:T(8,128)(2,1)}, u32[]{:S(2)}) copy-start(bf16[1024,2,64]{0,2,1:T(8,128)(2,1)} %param.18) | copy-start | bytes 786436
  519.2 59.2 %all-to-all-start.3 = ((bf16[64,16,1024]{2,1,0:T(8,128)(2,1)}), bf16[64,16,1024]{2,1,0:T(8,128)(2,1)}, u32[]{:S(2)}, u32[]{:S(2)}) async-start(bf16[64,16,1024]{2,1,0:T(8,128)(2,1)} %broadcast_select_fusion), calls=%async_computation.3 | async-start | bytes 4194304 | tf_op jit(solution)/shard_map/all_to_all | solution.py:196
  527.3 96.3 %reduce-scatter.2.cloned.1.call-start = ((), (), s32[]{:S(2)}) async-start(), calls=%async_computation.6 | async-start | bytes 2621440 | tf_op jit(solution)/shard_map/reduce_scatter | solution.py:207
  578.4 4.6 copy-start.14
  585.8 5.3 copy-start.16
  (16 other events, 18.3 us)
Sparse Core Ops, SparseCore 0:
  28.3 89.2 all-gather.5
  238.1 84.0 all-gather.3
  596.4 27.1 reduce-scatter.1
